TPU v7x, 256 devices: a whole 4x4x8 slice. The times are simulated.
256 devices in a mesh: seq: 32 (over y, x, core), head: 8 (over z).
Axes of the slice: x: 4, y: 4, z: 8, core: 2. Of those that a mesh axis runs over, the one named last changes fastest.
Arguments:
- queries: bfloat16 [32768, 8192], P(('seq', 'head')), may hold values from -6 to 6
- key_vectors: bfloat16 [32768, 8192], P(('seq', 'head')), may hold values from -6 to 6
- value_vectors: bfloat16 [32768, 8192], P(('seq', 'head')), may hold values from -6 to 6
- out_gain: float32 [64, 128], P('head'), may hold values from 0.1 to 1.9
Outputs:
- attended: bfloat16 [32768, 8192], P(('seq', 'head'))
All inputs are finite; a program needn't handle non-finite values.
Results may differ from a plain program's by a relative error of at most 0.0049.
Values may be sent and summed in bfloat16 or wider, within the bound.
A program may use at most 128 MiB of HBM per device.

v0:
```python
import jax
import jax.numpy as jnp
from jax import lax
from jax.sharding import PartitionSpec as P

HEADS = 64
HD = 128
BLOCK = 512


def passed_along(block, axis, distance):
    devices = range(lax.axis_size(axis))
    route = [(i - distance, i) for i in devices if i - distance in devices]
    return lax.ppermute(block, axis, route)


def split_heads(matrix):
    return matrix.reshape(matrix.shape[0], HEADS, HD)


def to_blocks(tensor):
    return tensor.reshape(tensor.shape[0] // BLOCK, BLOCK, tensor.shape[1], HD)


def block_states(key_heads, value_heads):
    return jnp.einsum(
        "nbhd,nbhe->nhde",
        to_blocks(key_heads),
        to_blocks(value_heads),
        preferred_element_type=jnp.float32,
    )


def carried_states(states):
    own = jnp.sum(states, axis=0)
    seq_count = lax.axis_size("seq")

    def relay(step, prefix):
        return passed_along(prefix + own, "seq", 1)

    prefix = lax.fori_loop(0, seq_count - 1, relay, jnp.zeros_like(own))
    carried = prefix[None] + (jnp.cumsum(states, axis=0) - states)
    return carried.astype(jnp.bfloat16)


def per_device(queries, key_vectors, value_vectors, out_gain):
    query_heads, key_heads, value_heads = (
        lax.all_to_all(split_heads(queries), "head", split_axis=1, concat_axis=0, tiled=True),
        lax.all_to_all(split_heads(key_vectors), "head", split_axis=1, concat_axis=0, tiled=True),
        lax.all_to_all(split_heads(value_vectors), "head", split_axis=1, concat_axis=0, tiled=True),
    )
    carried = carried_states(block_states(key_heads, value_heads))
    query_blocks = to_blocks(query_heads)
    key_blocks = to_blocks(key_heads)
    value_blocks = to_blocks(value_heads)
    inter = jnp.einsum("nbhd,nhde->nbhe", query_blocks, carried, preferred_element_type=jnp.float32)
    scores = jnp.einsum(
        "nbhd,nchd->nhbc", query_blocks, key_blocks, preferred_element_type=jnp.float32
    )
    causal = jnp.arange(BLOCK)[:, None] >= jnp.arange(BLOCK)[None, :]
    scores = jnp.where(causal[None, None], scores, jnp.float32(0.0)).astype(jnp.bfloat16)
    intra = jnp.einsum("nhbc,nchd->nbhd", scores, value_blocks, preferred_element_type=jnp.float32)
    raw = inter + intra
    scale = lax.rsqrt(jnp.mean(raw * raw, axis=-1, keepdims=True) + 1e-06)
    normed = (raw * scale * out_gain[None, None]).astype(jnp.bfloat16)
    normed = normed.reshape(query_heads.shape[0], query_heads.shape[1], HD)
    tokens_back = lax.all_to_all(normed, "head", split_axis=0, concat_axis=1, tiled=True)
    return tokens_back.reshape(tokens_back.shape[0], HEADS * HD)


def solution(mesh):
    return jax.shard_map(
        per_device,
        mesh=mesh,
        in_specs=(
            P(("seq", "head"), None),
            P(("seq", "head"), None),
            P(("seq", "head"), None),
            P("head", None),
        ),
        out_specs=P(("seq", "head"), None),
        check_vma=False,
    )
```

profile of v0, /device:TPU:16, one launch (start us, length us, event | category | flops | bytes accessed | tf_op | source)
XLA Modules:
  0.0 646.3 jit_solution(1137800084721814047)
XLA Ops:
  0.0 3.2 copy.45
  6.1 8.5 %all-to-all-start = ((bf16[128,64,128]{2,0,1:T(8,128)(2,1)}), bf16[128,64,128]{2,0,1:T(8,128)(2,1)S(1)}, u32[]{:S(2)}, u32[]{:S(2)}) async-start(bf16[128,64,128]{2,0,1:T(8,128)(2,1)} %copy.46), calls=%async_computation | async-start | bytes 4194304 | tf_op jit(solution)/shard_map/all_to_all | solution.py:49
  14.6 4.1 copy.49
  18.7 4.1 copy.50
  22.7 43.1 %all-to-all-done = bf16[128,64,128]{2,0,1:T(8,128)(2,1)S(1)} async-done(((bf16[128,64,128]{2,0,1:T(8,128)(2,1)}), bf16[128,64,128]{2,0,1:T(8,128)(2,1)S(1)}, u32[]{:S(2)}, u32[]{:S(2)}) %all-to-all-start) | async-done | bytes 2097184 | tf_op jit(solution)/shard_map/all_to_all | solution.py:49
  65.8 4.3 all-to-all-start.1
  70.1 4.1 copy.55
  74.2 4.1 copy.56
  78.3 43.5 %all-to-all-done.1 = bf16[128,64,128]{2,0,1:T(8,128)(2,1)} async-done(((bf16[128,64,128]{2,0,1:T(8,128)(2,1)}), bf16[128,64,128]{2,0,1:T(8,128)(2,1)}, u32[]{:S(2)}, u32[]{:S(2)}) %all-to-all-start.1) | async-done | bytes 2097184 | tf_op jit(solution)/shard_map/all_to_all | solution.py:50
  121.8 4.4 all-to-all-start.2
  132.0 43.0 %all-to-all-done.2 = bf16[128,64,128]{2,0,1:T(8,128)(2,1)} async-done(((bf16[128,64,128]{2,0,1:T(8,128)(2,1)}), bf16[128,64,128]{2,0,1:T(8,128)(2,1)}, u32[]{:S(2)}, u32[]{:S(2)}) %all-to-all-start.2) | async-done | bytes 2097184 | tf_op jit(solution)/shard_map/all_to_all | solution.py:48
  175.0 4.4 copy.58
  181.6 392.8 %while.10 = (s32[]{:T(128)}, f32[8,128,128]{2,1,0:T(8,128)S(1)}, f32[8,128,128]{2,1,0:T(8,128)S(1)}, s32[]{:T(128)}) while((s32[]{:T(128)}, f32[8,128,128]{2,1,0:T(8,128)S(1)}, f32[8,128,128]{2,1,0:T(8,128)S(1)}, s32[]{:T(128)}) %tuple.20), condition=%wide.region_2.0_spmd, body=%wide.region_1.0_spmd.sunk | while | flops 131074 | bytes 3670109 | solution.py:41
  183.6 10.7 %collective-permute-done = f32[8,128,128]{2,1,0:T(8,128)S(1)} collective-permute-done((f32[8,128,128]{2,1,0:T(8,128)S(1)}, f32[8,128,128]{2,1,0:T(8,128)S(1)}, u32[]{:S(2)}, u32[]{:S(2)}) %collective-permute-start) | collective-permute-done | bytes 524320 | tf_op jit(solution)/shard_map/while/body/eval_jaxpr/ppermute | solution.py:14
  196.3 10.7 %collective-permute-done = f32[8,128,128]{2,1,0:T(8,128)S(1)} collective-permute-done((f32[8,128,128]{2,1,0:T(8,128)S(1)}, f32[8,128,128]{2,1,0:T(8,128)S(1)}, u32[]{:S(2)}, u32[]{:S(2)}) %collective-permute-start) | collective-permute-done | bytes 524320 | tf_op jit(solution)/shard_map/while/body/eval_jaxpr/ppermute | solution.py:14
  209.0 10.7 %collective-permute-done = f32[8,128,128]{2,1,0:T(8,128)S(1)} collective-permute-done((f32[8,128,128]{2,1,0:T(8,128)S(1)}, f32[8,128,128]{2,1,0:T(8,128)S(1)}, u32[]{:S(2)}, u32[]{:S(2)}) %collective-permute-start) | collective-permute-done | bytes 524320 | tf_op jit(solution)/shard_map/while/body/eval_jaxpr/ppermute | solution.py:14
  221.6 10.7 %collective-permute-done = f32[8,128,128]{2,1,0:T(8,128)S(1)} collective-permute-done((f32[8,128,128]{2,1,0:T(8,128)S(1)}, f32[8,128,128]{2,1,0:T(8,128)S(1)}, u32[]{:S(2)}, u32[]{:S(2)}) %collective-permute-start) | collective-permute-done | bytes 524320 | tf_op jit(solution)/shard_map/while/body/eval_jaxpr/ppermute | solution.py:14
  234.3 10.7 %collective-permute-done = f32[8,128,128]{2,1,0:T(8,128)S(1)} collective-permute-done((f32[8,128,128]{2,1,0:T(8,128)S(1)}, f32[8,128,128]{2,1,0:T(8,128)S(1)}, u32[]{:S(2)}, u32[]{:S(2)}) %collective-permute-start) | collective-permute-done | bytes 524320 | tf_op jit(solution)/shard_map/while/body/eval_jaxpr/ppermute | solution.py:14
  247.0 10.7 %collective-permute-done = f32[8,128,128]{2,1,0:T(8,128)S(1)} collective-permute-done((f32[8,128,128]{2,1,0:T(8,128)S(1)}, f32[8,128,128]{2,1,0:T(8,128)S(1)}, u32[]{:S(2)}, u32[]{:S(2)}) %collective-permute-start) | collective-permute-done | bytes 524320 | tf_op jit(solution)/shard_map/while/body/eval_jaxpr/ppermute | solution.py:14
  259.7 10.7 %collective-permute-done = f32[8,128,128]{2,1,0:T(8,128)S(1)} collective-permute-done((f32[8,128,128]{2,1,0:T(8,128)S(1)}, f32[8,128,128]{2,1,0:T(8,128)S(1)}, u32[]{:S(2)}, u32[]{:S(2)}) %collective-permute-start) | collective-permute-done | bytes 524320 | tf_op jit(solution)/shard_map/while/body/eval_jaxpr/ppermute | solution.py:14
  272.3 10.7 %collective-permute-done = f32[8,128,128]{2,1,0:T(8,128)S(1)} collective-permute-done((f32[8,128,128]{2,1,0:T(8,128)S(1)}, f32[8,128,128]{2,1,0:T(8,128)S(1)}, u32[]{:S(2)}, u32[]{:S(2)}) %collective-permute-start) | collective-permute-done | bytes 524320 | tf_op jit(solution)/shard_map/while/body/eval_jaxpr/ppermute | solution.py:14
  285.0 10.7 %collective-permute-done = f32[8,128,128]{2,1,0:T(8,128)S(1)} collective-permute-done((f32[8,128,128]{2,1,0:T(8,128)S(1)}, f32[8,128,128]{2,1,0:T(8,128)S(1)}, u32[]{:S(2)}, u32[]{:S(2)}) %collective-permute-start) | collective-permute-done | bytes 524320 | tf_op jit(solution)/shard_map/while/body/eval_jaxpr/ppermute | solution.py:14
  297.7 10.7 %collective-permute-done = f32[8,128,128]{2,1,0:T(8,128)S(1)} collective-permute-done((f32[8,128,128]{2,1,0:T(8,128)S(1)}, f32[8,128,128]{2,1,0:T(8,128)S(1)}, u32[]{:S(2)}, u32[]{:S(2)}) %collective-permute-start) | collective-permute-done | bytes 524320 | tf_op jit(solution)/shard_map/while/body/eval_jaxpr/ppermute | solution.py:14
  310.3 10.7 %collective-permute-done = f32[8,128,128]{2,1,0:T(8,128)S(1)} collective-permute-done((f32[8,128,128]{2,1,0:T(8,128)S(1)}, f32[8,128,128]{2,1,0:T(8,128)S(1)}, u32[]{:S(2)}, u32[]{:S(2)}) %collective-permute-start) | collective-permute-done | bytes 524320 | tf_op jit(solution)/shard_map/while/body/eval_jaxpr/ppermute | solution.py:14
  323.0 10.7 %collective-permute-done = f32[8,128,128]{2,1,0:T(8,128)S(1)} collective-permute-done((f32[8,128,128]{2,1,0:T(8,128)S(1)}, f32[8,128,128]{2,1,0:T(8,128)S(1)}, u32[]{:S(2)}, u32[]{:S(2)}) %collective-permute-start) | collective-permute-done | bytes 524320 | tf_op jit(solution)/shard_map/while/body/eval_jaxpr/ppermute | solution.py:14
  335.7 10.7 %collective-permute-done = f32[8,128,128]{2,1,0:T(8,128)S(1)} collective-permute-done((f32[8,128,128]{2,1,0:T(8,128)S(1)}, f32[8,128,128]{2,1,0:T(8,128)S(1)}, u32[]{:S(2)}, u32[]{:S(2)}) %collective-permute-start) | collective-permute-done | bytes 524320 | tf_op jit(solution)/shard_map/while/body/eval_jaxpr/ppermute | solution.py:14
  348.3 10.7 %collective-permute-done = f32[8,128,128]{2,1,0:T(8,128)S(1)} collective-permute-done((f32[8,128,128]{2,1,0:T(8,128)S(1)}, f32[8,128,128]{2,1,0:T(8,128)S(1)}, u32[]{:S(2)}, u32[]{:S(2)}) %collective-permute-start) | collective-permute-done | bytes 524320 | tf_op jit(solution)/shard_map/while/body/eval_jaxpr/ppermute | solution.py:14
  361.0 10.7 %collective-permute-done = f32[8,128,128]{2,1,0:T(8,128)S(1)} collective-permute-done((f32[8,128,128]{2,1,0:T(8,128)S(1)}, f32[8,128,128]{2,1,0:T(8,128)S(1)}, u32[]{:S(2)}, u32[]{:S(2)}) %collective-permute-start) | collective-permute-done | bytes 524320 | tf_op jit(solution)/shard_map/while/body/eval_jaxpr/ppermute | solution.py:14
  373.7 10.7 %collective-permute-done = f32[8,128,128]{2,1,0:T(8,128)S(1)} collective-permute-done((f32[8,128,128]{2,1,0:T(8,128)S(1)}, f32[8,128,128]{2,1,0:T(8,128)S(1)}, u32[]{:S(2)}, u32[]{:S(2)}) %collective-permute-start) | collective-permute-done | bytes 524320 | tf_op jit(solution)/shard_map/while/body/eval_jaxpr/ppermute | solution.py:14
  386.4 10.7 %collective-permute-done = f32[8,128,128]{2,1,0:T(8,128)S(1)} collective-permute-done((f32[8,128,128]{2,1,0:T(8,128)S(1)}, f32[8,128,128]{2,1,0:T(8,128)S(1)}, u32[]{:S(2)}, u32[]{:S(2)}) %collective-permute-start) | collective-permute-done | bytes 524320 | tf_op jit(solution)/shard_map/while/body/eval_jaxpr/ppermute | solution.py:14
  399.0 10.7 %collective-permute-done = f32[8,128,128]{2,1,0:T(8,128)S(1)} collective-permute-done((f32[8,128,128]{2,1,0:T(8,128)S(1)}, f32[8,128,128]{2,1,0:T(8,128)S(1)}, u32[]{:S(2)}, u32[]{:S(2)}) %collective-permute-start) | collective-permute-done | bytes 524320 | tf_op jit(solution)/shard_map/while/body/eval_jaxpr/ppermute | solution.py:14
  411.7 10.7 %collective-permute-done = f32[8,128,128]{2,1,0:T(8,128)S(1)} collective-permute-done((f32[8,128,128]{2,1,0:T(8,128)S(1)}, f32[8,128,128]{2,1,0:T(8,128)S(1)}, u32[]{:S(2)}, u32[]{:S(2)}) %collective-permute-start) | collective-permute-done | bytes 524320 | tf_op jit(solution)/shard_map/while/body/eval_jaxpr/ppermute | solution.py:14
  424.4 10.7 %collective-permute-done = f32[8,128,128]{2,1,0:T(8,128)S(1)} collective-permute-done((f32[8,128,128]{2,1,0:T(8,128)S(1)}, f32[8,128,128]{2,1,0:T(8,128)S(1)}, u32[]{:S(2)}, u32[]{:S(2)}) %collective-permute-start) | collective-permute-done | bytes 524320 | tf_op jit(solution)/shard_map/while/body/eval_jaxpr/ppermute | solution.py:14
  437.0 10.7 %collective-permute-done = f32[8,128,128]{2,1,0:T(8,128)S(1)} collective-permute-done((f32[8,128,128]{2,1,0:T(8,128)S(1)}, f32[8,128,128]{2,1,0:T(8,128)S(1)}, u32[]{:S(2)}, u32[]{:S(2)}) %collective-permute-start) | collective-permute-done | bytes 524320 | tf_op jit(solution)/shard_map/while/body/eval_jaxpr/ppermute | solution.py:14
  449.7 10.7 %collective-permute-done = f32[8,128,128]{2,1,0:T(8,128)S(1)} collective-permute-done((f32[8,128,128]{2,1,0:T(8,128)S(1)}, f32[8,128,128]{2,1,0:T(8,128)S(1)}, u32[]{:S(2)}, u32[]{:S(2)}) %collective-permute-start) | collective-permute-done | bytes 524320 | tf_op jit(solution)/shard_map/while/body/eval_jaxpr/ppermute | solution.py:14
  462.4 10.7 %collective-permute-done = f32[8,128,128]{2,1,0:T(8,128)S(1)} collective-permute-done((f32[8,128,128]{2,1,0:T(8,128)S(1)}, f32[8,128,128]{2,1,0:T(8,128)S(1)}, u32[]{:S(2)}, u32[]{:S(2)}) %collective-permute-start) | collective-permute-done | bytes 524320 | tf_op jit(solution)/shard_map/while/body/eval_jaxpr/ppermute | solution.py:14
  475.0 10.7 %collective-permute-done = f32[8,128,128]{2,1,0:T(8,128)S(1)} collective-permute-done((f32[8,128,128]{2,1,0:T(8,128)S(1)}, f32[8,128,128]{2,1,0:T(8,128)S(1)}, u32[]{:S(2)}, u32[]{:S(2)}) %collective-permute-start) | collective-permute-done | bytes 524320 | tf_op jit(solution)/shard_map/while/body/eval_jaxpr/ppermute | solution.py:14
  487.7 10.7 %collective-permute-done = f32[8,128,128]{2,1,0:T(8,128)S(1)} collective-permute-done((f32[8,128,128]{2,1,0:T(8,128)S(1)}, f32[8,128,128]{2,1,0:T(8,128)S(1)}, u32[]{:S(2)}, u32[]{:S(2)}) %collective-permute-start) | collective-permute-done | bytes 524320 | tf_op jit(solution)/shard_map/while/body/eval_jaxpr/ppermute | solution.py:14
  500.4 10.7 %collective-permute-done = f32[8,128,128]{2,1,0:T(8,128)S(1)} collective-permute-done((f32[8,128,128]{2,1,0:T(8,128)S(1)}, f32[8,128,128]{2,1,0:T(8,128)S(1)}, u32[]{:S(2)}, u32[]{:S(2)}) %collective-permute-start) | collective-permute-done | bytes 524320 | tf_op jit(solution)/shard_map/while/body/eval_jaxpr/ppermute | solution.py:14
  513.1 10.7 %collective-permute-done = f32[8,128,128]{2,1,0:T(8,128)S(1)} collective-permute-done((f32[8,128,128]{2,1,0:T(8,128)S(1)}, f32[8,128,128]{2,1,0:T(8,128)S(1)}, u32[]{:S(2)}, u32[]{:S(2)}) %collective-permute-start) | collective-permute-done | bytes 524320 | tf_op jit(solution)/shard_map/while/body/eval_jaxpr/ppermute | solution.py:14
  525.7 10.7 %collective-permute-done = f32[8,128,128]{2,1,0:T(8,128)S(1)} collective-permute-done((f32[8,128,128]{2,1,0:T(8,128)S(1)}, f32[8,128,128]{2,1,0:T(8,128)S(1)}, u32[]{:S(2)}, u32[]{:S(2)}) %collective-permute-start) | collective-permute-done | bytes 524320 | tf_op jit(solution)/shard_map/while/body/eval_jaxpr/ppermute | solution.py:14
  538.4 10.7 %collective-permute-done = f32[8,128,128]{2,1,0:T(8,128)S(1)} collective-permute-done((f32[8,128,128]{2,1,0:T(8,128)S(1)}, f32[8,128,128]{2,1,0:T(8,128)S(1)}, u32[]{:S(2)}, u32[]{:S(2)}) %collective-permute-start) | collective-permute-done | bytes 524320 | tf_op jit(solution)/shard_map/while/body/eval_jaxpr/ppermute | solution.py:14
  551.1 10.7 %collective-permute-done = f32[8,128,128]{2,1,0:T(8,128)S(1)} collective-permute-done((f32[8,128,128]{2,1,0:T(8,128)S(1)}, f32[8,128,128]{2,1,0:T(8,128)S(1)}, u32[]{:S(2)}, u32[]{:S(2)}) %collective-permute-start) | collective-permute-done | bytes 524320 | tf_op jit(solution)/shard_map/while/body/eval_jaxpr/ppermute | solution.py:14
  563.7 10.7 %collective-permute-done = f32[8,128,128]{2,1,0:T(8,128)S(1)} collective-permute-done((f32[8,128,128]{2,1,0:T(8,128)S(1)}, f32[8,128,128]{2,1,0:T(8,128)S(1)}, u32[]{:S(2)}, u32[]{:S(2)}) %collective-permute-start) | collective-permute-done | bytes 524320 | tf_op jit(solution)/shard_map/while/body/eval_jaxpr/ppermute | solution.py:14
  576.6 9.2 %fusion = f32[2,8,512,128]{2,3,1,0:T(8,128)} fusion(pred[512,512]{1,0:T(8,128)(4,1)S(1)} %iota_compare_fusion, bf16[2,512,8,128]{3,2,1,0:T(8,128)(2,1)} %bitcast.35, bf16[2,512,8,128]{3,2,1,0:T(8,128)(2,1)S(1)} %bitcast.33, bf16[2,512,8,128]{3,2,1,0:T(8,128)(2,1)} %bitcast.38), kind=kOutput, calls=%fused_computation.1 | convolution fusion | flops 2155872256 | bytes 10747904 | tf_op jit(solution)/shard_map/nhbc,nchd->nbhd/dot_general | solution.py:62
  585.9 3.2 multiply_reduce_fusion
  594.1 46.0 %all_to_all.60 = bf16[1024,8,128]{2,1,0:T(8,128)(2,1)} all-to-all(bf16[1024,8,128]{2,1,0:T(8,128)(2,1)S(1)} %bitcast.27), channel_id=1, replica_groups=mesh['seq'=32,'head'=8] {'head'}, dimensions={0} | all-to-all | bytes 4194304 | tf_op jit(solution)/shard_map/all_to_all | solution.py:67
  640.1 3.3 copy.66
  (81 shorter events, 82.2 us)
Async XLA Ops:
  6.1 59.7 %all-to-all-start = ((bf16[128,64,128]{2,0,1:T(8,128)(2,1)}), bf16[128,64,128]{2,0,1:T(8,128)(2,1)S(1)}, u32[]{:S(2)}, u32[]{:S(2)}) async-start(bf16[128,64,128]{2,0,1:T(8,128)(2,1)} %copy.46), calls=%async_computation | async-start | bytes 4194304 | tf_op jit(solution)/shard_map/all_to_all | solution.py:49
  65.8 56.0 %all-to-all-start.1 = ((bf16[128,64,128]{2,0,1:T(8,128)(2,1)}), bf16[128,64,128]{2,0,1:T(8,128)(2,1)}, u32[]{:S(2)}, u32[]{:S(2)}) async-start(bf16[128,64,128]{2,0,1:T(8,128)(2,1)} %copy.50), calls=%async_computation.1 | async-start | bytes 4194304 | tf_op jit(solution)/shard_map/all_to_all | solution.py:50
  121.8 53.2 %all-to-all-start.2 = ((bf16[128,64,128]{2,0,1:T(8,128)(2,1)}), bf16[128,64,128]{2,0,1:T(8,128)(2,1)}, u32[]{:S(2)}, u32[]{:S(2)}) async-start(bf16[128,64,128]{2,0,1:T(8,128)(2,1)} %copy.56), calls=%async_computation.2 | async-start | bytes 4194304 | tf_op jit(solution)/shard_map/all_to_all | solution.py:48
  131.9 47.5 %copy-start.2 = (bf16[8,128,8,128]{3,2,1,0:T(8,128)(2,1)}, bf16[8,128,8,128]{3,2,1,0:T(8,128)(2,1)S(1)}, u32[]{:S(2)}) copy-start(bf16[8,128,8,128]{3,2,1,0:T(8,128)(2,1)S(1)} %copy.52) | copy-start | bytes 6291460
  175.0 4.5 copy-start.1
  181.7 12.6 %collective-permute-start = (f32[8,128,128]{2,1,0:T(8,128)S(1)}, f32[8,128,128]{2,1,0:T(8,128)S(1)}, u32[]{:S(2)}, u32[]{:S(2)}) collective-permute-start(f32[8,128,128]{2,1,0:T(8,128)S(1)} %add.43), channel_id=1, source_target_pairs={{0,8},{8,16},{16,24},{24,32},{32,40},{40,48},{48,56},{56,64},{64,7... | collective-permute-start | bytes 1572872 | tf_op jit(solution)/shard_map/while/body/eval_jaxpr/ppermute | solution.py:14
  194.4 12.6 %collective-permute-start = (f32[8,128,128]{2,1,0:T(8,128)S(1)}, f32[8,128,128]{2,1,0:T(8,128)S(1)}, u32[]{:S(2)}, u32[]{:S(2)}) collective-permute-start(f32[8,128,128]{2,1,0:T(8,128)S(1)} %add.43), channel_id=1, source_target_pairs={{0,8},{8,16},{16,24},{24,32},{32,40},{40,48},{48,56},{56,64},{64,7... | collective-permute-start | bytes 1572872 | tf_op jit(solution)/shard_map/while/body/eval_jaxpr/ppermute | solution.py:14
  207.0 12.6 %collective-permute-start = (f32[8,128,128]{2,1,0:T(8,128)S(1)}, f32[8,128,128]{2,1,0:T(8,128)S(1)}, u32[]{:S(2)}, u32[]{:S(2)}) collective-permute-start(f32[8,128,128]{2,1,0:T(8,128)S(1)} %add.43), channel_id=1, source_target_pairs={{0,8},{8,16},{16,24},{24,32},{32,40},{40,48},{48,56},{56,64},{64,7... | collective-permute-start | bytes 1572872 | tf_op jit(solution)/shard_map/while/body/eval_jaxpr/ppermute | solution.py:14
  219.7 12.6 %collective-permute-start = (f32[8,128,128]{2,1,0:T(8,128)S(1)}, f32[8,128,128]{2,1,0:T(8,128)S(1)}, u32[]{:S(2)}, u32[]{:S(2)}) collective-permute-start(f32[8,128,128]{2,1,0:T(8,128)S(1)} %add.43), channel_id=1, source_target_pairs={{0,8},{8,16},{16,24},{24,32},{32,40},{40,48},{48,56},{56,64},{64,7... | collective-permute-start | bytes 1572872 | tf_op jit(solution)/shard_map/while/body/eval_jaxpr/ppermute | solution.py:14
  232.4 12.6 %collective-permute-start = (f32[8,128,128]{2,1,0:T(8,128)S(1)}, f32[8,128,128]{2,1,0:T(8,128)S(1)}, u32[]{:S(2)}, u32[]{:S(2)}) collective-permute-start(f32[8,128,128]{2,1,0:T(8,128)S(1)} %add.43), channel_id=1, source_target_pairs={{0,8},{8,16},{16,24},{24,32},{32,40},{40,48},{48,56},{56,64},{64,7... | collective-permute-start | bytes 1572872 | tf_op jit(solution)/shard_map/while/body/eval_jaxpr/ppermute | solution.py:14
  245.1 12.6 %collective-permute-start = (f32[8,128,128]{2,1,0:T(8,128)S(1)}, f32[8,128,128]{2,1,0:T(8,128)S(1)}, u32[]{:S(2)}, u32[]{:S(2)}) collective-permute-start(f32[8,128,128]{2,1,0:T(8,128)S(1)} %add.43), channel_id=1, source_target_pairs={{0,8},{8,16},{16,24},{24,32},{32,40},{40,48},{48,56},{56,64},{64,7... | collective-permute-start | bytes 1572872 | tf_op jit(solution)/shard_map/while/body/eval_jaxpr/ppermute | solution.py:14
  257.7 12.6 %collective-permute-start = (f32[8,128,128]{2,1,0:T(8,128)S(1)}, f32[8,128,128]{2,1,0:T(8,128)S(1)}, u32[]{:S(2)}, u32[]{:S(2)}) collective-permute-start(f32[8,128,128]{2,1,0:T(8,128)S(1)} %add.43), channel_id=1, source_target_pairs={{0,8},{8,16},{16,24},{24,32},{32,40},{40,48},{48,56},{56,64},{64,7... | collective-permute-start | bytes 1572872 | tf_op jit(solution)/shard_map/while/body/eval_jaxpr/ppermute | solution.py:14
  270.4 12.6 %collective-permute-start = (f32[8,128,128]{2,1,0:T(8,128)S(1)}, f32[8,128,128]{2,1,0:T(8,128)S(1)}, u32[]{:S(2)}, u32[]{:S(2)}) collective-permute-start(f32[8,128,128]{2,1,0:T(8,128)S(1)} %add.43), channel_id=1, source_target_pairs={{0,8},{8,16},{16,24},{24,32},{32,40},{40,48},{48,56},{56,64},{64,7... | collective-permute-start | bytes 1572872 | tf_op jit(solution)/shard_map/while/body/eval_jaxpr/ppermute | solution.py:14
  283.1 12.6 %collective-permute-start = (f32[8,128,128]{2,1,0:T(8,128)S(1)}, f32[8,128,128]{2,1,0:T(8,128)S(1)}, u32[]{:S(2)}, u32[]{:S(2)}) collective-permute-start(f32[8,128,128]{2,1,0:T(8,128)S(1)} %add.43), channel_id=1, source_target_pairs={{0,8},{8,16},{16,24},{24,32},{32,40},{40,48},{48,56},{56,64},{64,7... | collective-permute-start | bytes 1572872 | tf_op jit(solution)/shard_map/while/body/eval_jaxpr/ppermute | solution.py:14
  295.7 12.6 %collective-permute-start = (f32[8,128,128]{2,1,0:T(8,128)S(1)}, f32[8,128,128]{2,1,0:T(8,128)S(1)}, u32[]{:S(2)}, u32[]{:S(2)}) collective-permute-start(f32[8,128,128]{2,1,0:T(8,128)S(1)} %add.43), channel_id=1, source_target_pairs={{0,8},{8,16},{16,24},{24,32},{32,40},{40,48},{48,56},{56,64},{64,7... | collective-permute-start | bytes 1572872 | tf_op jit(solution)/shard_map/while/body/eval_jaxpr/ppermute | solution.py:14
  308.4 12.6 %collective-permute-start = (f32[8,128,128]{2,1,0:T(8,128)S(1)}, f32[8,128,128]{2,1,0:T(8,128)S(1)}, u32[]{:S(2)}, u32[]{:S(2)}) collective-permute-start(f32[8,128,128]{2,1,0:T(8,128)S(1)} %add.43), channel_id=1, source_target_pairs={{0,8},{8,16},{16,24},{24,32},{32,40},{40,48},{48,56},{56,64},{64,7... | collective-permute-start | bytes 1572872 | tf_op jit(solution)/shard_map/while/body/eval_jaxpr/ppermute | solution.py:14
  321.1 12.6 %collective-permute-start = (f32[8,128,128]{2,1,0:T(8,128)S(1)}, f32[8,128,128]{2,1,0:T(8,128)S(1)}, u32[]{:S(2)}, u32[]{:S(2)}) collective-permute-start(f32[8,128,128]{2,1,0:T(8,128)S(1)} %add.43), channel_id=1, source_target_pairs={{0,8},{8,16},{16,24},{24,32},{32,40},{40,48},{48,56},{56,64},{64,7... | collective-permute-start | bytes 1572872 | tf_op jit(solution)/shard_map/while/body/eval_jaxpr/ppermute | solution.py:14
  333.7 12.6 %collective-permute-start = (f32[8,128,128]{2,1,0:T(8,128)S(1)}, f32[8,128,128]{2,1,0:T(8,128)S(1)}, u32[]{:S(2)}, u32[]{:S(2)}) collective-permute-start(f32[8,128,128]{2,1,0:T(8,128)S(1)} %add.43), channel_id=1, source_target_pairs={{0,8},{8,16},{16,24},{24,32},{32,40},{40,48},{48,56},{56,64},{64,7... | collective-permute-start | bytes 1572872 | tf_op jit(solution)/shard_map/while/body/eval_jaxpr/ppermute | solution.py:14
  346.4 12.6 %collective-permute-start = (f32[8,128,128]{2,1,0:T(8,128)S(1)}, f32[8,128,128]{2,1,0:T(8,128)S(1)}, u32[]{:S(2)}, u32[]{:S(2)}) collective-permute-start(f32[8,128,128]{2,1,0:T(8,128)S(1)} %add.43), channel_id=1, source_target_pairs={{0,8},{8,16},{16,24},{24,32},{32,40},{40,48},{48,56},{56,64},{64,7... | collective-permute-start | bytes 1572872 | tf_op jit(solution)/shard_map/while/body/eval_jaxpr/ppermute | solution.py:14
  359.1 12.6 %collective-permute-start = (f32[8,128,128]{2,1,0:T(8,128)S(1)}, f32[8,128,128]{2,1,0:T(8,128)S(1)}, u32[]{:S(2)}, u32[]{:S(2)}) collective-permute-start(f32[8,128,128]{2,1,0:T(8,128)S(1)} %add.43), channel_id=1, source_target_pairs={{0,8},{8,16},{16,24},{24,32},{32,40},{40,48},{48,56},{56,64},{64,7... | collective-permute-start | bytes 1572872 | tf_op jit(solution)/shard_map/while/body/eval_jaxpr/ppermute | solution.py:14
  371.8 12.6 %collective-permute-start = (f32[8,128,128]{2,1,0:T(8,128)S(1)}, f32[8,128,128]{2,1,0:T(8,128)S(1)}, u32[]{:S(2)}, u32[]{:S(2)}) collective-permute-start(f32[8,128,128]{2,1,0:T(8,128)S(1)} %add.43), channel_id=1, source_target_pairs={{0,8},{8,16},{16,24},{24,32},{32,40},{40,48},{48,56},{56,64},{64,7... | collective-permute-start | bytes 1572872 | tf_op jit(solution)/shard_map/while/body/eval_jaxpr/ppermute | solution.py:14
  384.4 12.6 %collective-permute-start = (f32[8,128,128]{2,1,0:T(8,128)S(1)}, f32[8,128,128]{2,1,0:T(8,128)S(1)}, u32[]{:S(2)}, u32[]{:S(2)}) collective-permute-start(f32[8,128,128]{2,1,0:T(8,128)S(1)} %add.43), channel_id=1, source_target_pairs={{0,8},{8,16},{16,24},{24,32},{32,40},{40,48},{48,56},{56,64},{64,7... | collective-permute-start | bytes 1572872 | tf_op jit(solution)/shard_map/while/body/eval_jaxpr/ppermute | solution.py:14
  397.1 12.6 %collective-permute-start = (f32[8,128,128]{2,1,0:T(8,128)S(1)}, f32[8,128,128]{2,1,0:T(8,128)S(1)}, u32[]{:S(2)}, u32[]{:S(2)}) collective-permute-start(f32[8,128,128]{2,1,0:T(8,128)S(1)} %add.43), channel_id=1, source_target_pairs={{0,8},{8,16},{16,24},{24,32},{32,40},{40,48},{48,56},{56,64},{64,7... | collective-permute-start | bytes 1572872 | tf_op jit(solution)/shard_map/while/body/eval_jaxpr/ppermute | solution.py:14
  409.8 12.6 %collective-permute-start = (f32[8,128,128]{2,1,0:T(8,128)S(1)}, f32[8,128,128]{2,1,0:T(8,128)S(1)}, u32[]{:S(2)}, u32[]{:S(2)}) collective-permute-start(f32[8,128,128]{2,1,0:T(8,128)S(1)} %add.43), channel_id=1, source_target_pairs={{0,8},{8,16},{16,24},{24,32},{32,40},{40,48},{48,56},{56,64},{64,7... | collective-permute-start | bytes 1572872 | tf_op jit(solution)/shard_map/while/body/eval_jaxpr/ppermute | solution.py:14
  422.4 12.6 %collective-permute-start = (f32[8,128,128]{2,1,0:T(8,128)S(1)}, f32[8,128,128]{2,1,0:T(8,128)S(1)}, u32[]{:S(2)}, u32[]{:S(2)}) collective-permute-start(f32[8,128,128]{2,1,0:T(8,128)S(1)} %add.43), channel_id=1, source_target_pairs={{0,8},{8,16},{16,24},{24,32},{32,40},{40,48},{48,56},{56,64},{64,7... | collective-permute-start | bytes 1572872 | tf_op jit(solution)/shard_map/while/body/eval_jaxpr/ppermute | solution.py:14
  435.1 12.6 %collective-permute-start = (f32[8,128,128]{2,1,0:T(8,128)S(1)}, f32[8,128,128]{2,1,0:T(8,128)S(1)}, u32[]{:S(2)}, u32[]{:S(2)}) collective-permute-start(f32[8,128,128]{2,1,0:T(8,128)S(1)} %add.43), channel_id=1, source_target_pairs={{0,8},{8,16},{16,24},{24,32},{32,40},{40,48},{48,56},{56,64},{64,7... | collective-permute-start | bytes 1572872 | tf_op jit(solution)/shard_map/while/body/eval_jaxpr/ppermute | solution.py:14
  447.8 12.6 %collective-permute-start = (f32[8,128,128]{2,1,0:T(8,128)S(1)}, f32[8,128,128]{2,1,0:T(8,128)S(1)}, u32[]{:S(2)}, u32[]{:S(2)}) collective-permute-start(f32[8,128,128]{2,1,0:T(8,128)S(1)} %add.43), channel_id=1, source_target_pairs={{0,8},{8,16},{16,24},{24,32},{32,40},{40,48},{48,56},{56,64},{64,7... | collective-permute-start | bytes 1572872 | tf_op jit(solution)/shard_map/while/body/eval_jaxpr/ppermute | solution.py:14
  460.4 12.6 %collective-permute-start = (f32[8,128,128]{2,1,0:T(8,128)S(1)}, f32[8,128,128]{2,1,0:T(8,128)S(1)}, u32[]{:S(2)}, u32[]{:S(2)}) collective-permute-start(f32[8,128,128]{2,1,0:T(8,128)S(1)} %add.43), channel_id=1, source_target_pairs={{0,8},{8,16},{16,24},{24,32},{32,40},{40,48},{48,56},{56,64},{64,7... | collective-permute-start | bytes 1572872 | tf_op jit(solution)/shard_map/while/body/eval_jaxpr/ppermute | solution.py:14
  473.1 12.6 %collective-permute-start = (f32[8,128,128]{2,1,0:T(8,128)S(1)}, f32[8,128,128]{2,1,0:T(8,128)S(1)}, u32[]{:S(2)}, u32[]{:S(2)}) collective-permute-start(f32[8,128,128]{2,1,0:T(8,128)S(1)} %add.43), channel_id=1, source_target_pairs={{0,8},{8,16},{16,24},{24,32},{32,40},{40,48},{48,56},{56,64},{64,7... | collective-permute-start | bytes 1572872 | tf_op jit(solution)/shard_map/while/body/eval_jaxpr/ppermute | solution.py:14
  485.8 12.6 %collective-permute-start = (f32[8,128,128]{2,1,0:T(8,128)S(1)}, f32[8,128,128]{2,1,0:T(8,128)S(1)}, u32[]{:S(2)}, u32[]{:S(2)}) collective-permute-start(f32[8,128,128]{2,1,0:T(8,128)S(1)} %add.43), channel_id=1, source_target_pairs={{0,8},{8,16},{16,24},{24,32},{32,40},{40,48},{48,56},{56,64},{64,7... | collective-permute-start | bytes 1572872 | tf_op jit(solution)/shard_map/while/body/eval_jaxpr/ppermute | solution.py:14
  498.5 12.6 %collective-permute-start = (f32[8,128,128]{2,1,0:T(8,128)S(1)}, f32[8,128,128]{2,1,0:T(8,128)S(1)}, u32[]{:S(2)}, u32[]{:S(2)}) collective-permute-start(f32[8,128,128]{2,1,0:T(8,128)S(1)} %add.43), channel_id=1, source_target_pairs={{0,8},{8,16},{16,24},{24,32},{32,40},{40,48},{48,56},{56,64},{64,7... | collective-permute-start | bytes 1572872 | tf_op jit(solution)/shard_map/while/body/eval_jaxpr/ppermute | solution.py:14
  511.1 12.6 %collective-permute-start = (f32[8,128,128]{2,1,0:T(8,128)S(1)}, f32[8,128,128]{2,1,0:T(8,128)S(1)}, u32[]{:S(2)}, u32[]{:S(2)}) collective-permute-start(f32[8,128,128]{2,1,0:T(8,128)S(1)} %add.43), channel_id=1, source_target_pairs={{0,8},{8,16},{16,24},{24,32},{32,40},{40,48},{48,56},{56,64},{64,7... | collective-permute-start | bytes 1572872 | tf_op jit(solution)/shard_map/while/body/eval_jaxpr/ppermute | solution.py:14
  523.8 12.6 %collective-permute-start = (f32[8,128,128]{2,1,0:T(8,128)S(1)}, f32[8,128,128]{2,1,0:T(8,128)S(1)}, u32[]{:S(2)}, u32[]{:S(2)}) collective-permute-start(f32[8,128,128]{2,1,0:T(8,128)S(1)} %add.43), channel_id=1, source_target_pairs={{0,8},{8,16},{16,24},{24,32},{32,40},{40,48},{48,56},{56,64},{64,7... | collective-permute-start | bytes 1572872 | tf_op jit(solution)/shard_map/while/body/eval_jaxpr/ppermute | solution.py:14
  536.5 12.6 %collective-permute-start = (f32[8,128,128]{2,1,0:T(8,128)S(1)}, f32[8,128,128]{2,1,0:T(8,128)S(1)}, u32[]{:S(2)}, u32[]{:S(2)}) collective-permute-start(f32[8,128,128]{2,1,0:T(8,128)S(1)} %add.43), channel_id=1, source_target_pairs={{0,8},{8,16},{16,24},{24,32},{32,40},{40,48},{48,56},{56,64},{64,7... | collective-permute-start | bytes 1572872 | tf_op jit(solution)/shard_map/while/body/eval_jaxpr/ppermute | solution.py:14
  549.1 12.6 %collective-permute-start = (f32[8,128,128]{2,1,0:T(8,128)S(1)}, f32[8,128,128]{2,1,0:T(8,128)S(1)}, u32[]{:S(2)}, u32[]{:S(2)}) collective-permute-start(f32[8,128,128]{2,1,0:T(8,128)S(1)} %add.43), channel_id=1, source_target_pairs={{0,8},{8,16},{16,24},{24,32},{32,40},{40,48},{48,56},{56,64},{64,7... | collective-permute-start | bytes 1572872 | tf_op jit(solution)/shard_map/while/body/eval_jaxpr/ppermute | solution.py:14
  561.8 12.6 %collective-permute-start = (f32[8,128,128]{2,1,0:T(8,128)S(1)}, f32[8,128,128]{2,1,0:T(8,128)S(1)}, u32[]{:S(2)}, u32[]{:S(2)}) collective-permute-start(f32[8,128,128]{2,1,0:T(8,128)S(1)} %add.43), channel_id=1, source_target_pairs={{0,8},{8,16},{16,24},{24,32},{32,40},{40,48},{48,56},{56,64},{64,7... | collective-permute-start | bytes 1572872 | tf_op jit(solution)/shard_map/while/body/eval_jaxpr/ppermute | solution.py:14
  574.4 2.2 copy-start
  585.9 3.3 copy-start.3
where the time goes:
time: 648 us; the launch traced here: 646 us
  waiting for transfers between devices  461 us (71%)
  starting transfers between devices  76.7 us (12%)
  blocking collectives  46 us (7%)
  local copies, waits for them, and re-layouts  42.2 us (7%)
  matrix products  14.6 us (2%)
    ppermute x31, waiting for transfers between devices, passed_along(): return lax.ppermute(block, axis, route)  331 us
    ppermute x31, starting transfers between devices, passed_along(): return lax.ppermute(block, axis, route)  59.5 us
    all_to_all x1, blocking collectives, per_device(): lax.all_to_all(normed, 'head', split_axis=0, concat_axis=1, tiled=True)  46 us
    all_to_all x1, waiting for transfers between devices, per_device(): lax.all_to_all(split_heads(value_vectors), 'head', split_axis=1, concat_a...  43.5 us
    all_to_all x1, waiting for transfers between devices, per_device(): lax.all_to_all(split_heads(key_vectors), 'head', split_axis=1, concat_axi...  43.1 us
    all_to_all x1, waiting for transfers between devices, per_device(): lax.all_to_all(split_heads(queries), 'head', split_axis=1, concat_axis=0,...  43 us
  transfers between devices with their start and end apart: 34, of which 34 were waited for; matrix products, arithmetic and copies ran while one was open for 3% of the time, Pallas kernels for 0%

commit v1 on v0

v1 whole, which is shorter than its diff:
```python
import jax
import jax.numpy as jnp
from jax import lax
from jax.sharding import PartitionSpec as P

HEADS = 64
HD = 128


def shifted(block, axis, distance):
    count = lax.axis_size(axis)
    return lax.ppermute(block, axis, [(i, i + distance) for i in range(count - distance)])


def seq_exclusive(own):
    count = lax.axis_size("seq")
    total = own
    distance = 1
    while distance < count:
        total = total + shifted(total, "seq", distance)
        distance *= 2
    return shifted(total, "seq", 1)


def per_device(queries, key_vectors, value_vectors, out_gain):
    tokens = queries.shape[0]
    query_heads = queries.reshape(tokens, HEADS, HD)
    key_heads = key_vectors.reshape(tokens, HEADS, HD)
    value_heads = value_vectors.reshape(tokens, HEADS, HD)
    states = jnp.einsum("bhd,bhe->hde", key_heads, value_heads, preferred_element_type=jnp.float32)
    gathered = lax.all_to_all(
        states.astype(jnp.bfloat16).reshape(8, HEADS // 8, HD, HD), "head", split_axis=0, concat_axis=0, tiled=True
    ).astype(jnp.float32)
    gain = lax.all_gather(out_gain, "head", axis=0, tiled=True)
    prefix = seq_exclusive(jnp.sum(gathered, axis=0))
    running = prefix
    parts = []
    for z in range(8):
        parts.append(running.astype(jnp.bfloat16))
        running = running + gathered[z]
    carried = lax.all_to_all(jnp.stack(parts), "head", split_axis=0, concat_axis=0, tiled=True)
    carried = carried.reshape(HEADS, HD, HD)
    inter = jnp.einsum("bhd,hde->bhe", query_heads, carried, preferred_element_type=jnp.float32)
    scores = jnp.einsum("bhd,chd->hbc", query_heads, key_heads, preferred_element_type=jnp.float32)
    causal = jnp.arange(tokens)[:, None] >= jnp.arange(tokens)[None, :]
    scores = jnp.where(causal[None], scores, jnp.float32(0.0)).astype(jnp.bfloat16)
    intra = jnp.einsum("hbc,chd->bhd", scores, value_heads, preferred_element_type=jnp.float32)
    raw = inter + intra
    scale = lax.rsqrt(jnp.mean(raw * raw, axis=-1, keepdims=True) + 1e-06)
    normed = (raw * scale * gain[None]).astype(jnp.bfloat16)
    return normed.reshape(tokens, HEADS * HD)


def solution(mesh):
    return jax.shard_map(
        per_device,
        mesh=mesh,
        in_specs=(
            P(("seq", "head"), None),
            P(("seq", "head"), None),
            P(("seq", "head"), None),
            P("head", None),
        ),
        out_specs=P(("seq", "head"), None),
        check_vma=False,
    )
```

time: 648 us -> 248 us (0.38)
  waiting for transfers between devices: 461 us -> 64.8 us
  blocking collectives: 46 us -> 125 us
  starting transfers between devices: 76.7 us -> 17.2 us
  local copies, waits for them, and re-layouts: 42.2 us -> 12.3 us
    ppermute x31 -> x6, waiting for transfers between devices: 331 us -> 64.8 us  [shifted(): lax.ppermute(block, axis, [(i, i + distance) for i in range(count - dista...]
    all_to_all x3 -> x1, waiting for transfers between devices: 130 us -> 0.01 us  [per_device(): lax.all_to_all(jnp.stack(parts), 'head', split_axis=0, concat_axis=0, til...]
    all_gather x0 -> x1, blocking collectives: none -> 65.2 us  [per_device(): gain = lax.all_gather(out_gain, 'head', axis=0, tiled=True)]
    ppermute x31 -> x6, starting transfers between devices: 59.5 us -> 12.8 us  [shifted(): lax.ppermute(block, axis, [(i, i + distance) for i in range(count - dista...]
    all_to_all x1, blocking collectives: 46 us -> 59.5 us  [per_device(): lax.all_to_all(states.astype(jnp.bfloat16).reshape(8, HEADS // 8, HD, HD)...]
    all_to_all x4 -> x0, local copies, waits for them, and re-layouts: 13.4 us -> none  [the longest x1 4.44 us: per_device(): lax.all_to_all(split_heads(queries), 'head', split_axis=1, concat_axis=0,...]
    all_to_all x3 -> x1, starting transfers between devices: 17.2 us -> 4.47 us  [per_device(): lax.all_to_all(jnp.stack(parts), 'head', split_axis=0, concat_axis=0, til...]
    unnamed x11 -> x4, local copies, waits for them, and re-layouts: 11.7 us -> 0.01 us
  transfers between devices with their start and end apart: 34 -> 7, of which waited for: 34 -> 6; matrix products, arithmetic and copies ran while one was open for 3% -> 0% of each run, Pallas kernels for 0% -> 0%
where the time goes in v1:
time: 248 us; the launch traced here: 247 us
  blocking collectives  125 us (50%)
  waiting for transfers between devices  64.8 us (26%)
  starting transfers between devices  17.2 us (7%)
  matrix products  16.5 us (7%)
  local copies, waits for them, and re-layouts  12.3 us (5%)
  other arithmetic  11.3 us (5%)
    all_gather x1, blocking collectives, per_device(): gain = lax.all_gather(out_gain, 'head', axis=0, tiled=True)  65.2 us
    ppermute x6, waiting for transfers between devices, shifted(): lax.ppermute(block, axis, [(i, i + distance) for i in range(count - dista...  64.8 us
    all_to_all x1, blocking collectives, per_device(): lax.all_to_all(states.astype(jnp.bfloat16).reshape(8, HEADS // 8, HD, HD)...  59.5 us
    ppermute x6, starting transfers between devices, shifted(): lax.ppermute(block, axis, [(i, i + distance) for i in range(count - dista...  12.8 us
    dot_general x1, matrix products, per_device(): jnp.einsum('hbc,chd->bhd', scores, value_heads, preferred_element_type=jn...  7.56 us
    unnamed x7, other arithmetic  5.4 us
    dot_general x1, matrix products, per_device(): jnp.einsum('bhd,hde->bhe', query_heads, carried, preferred_element_type=j...  5.14 us
  transfers between devices with their start and end apart: 7, of which 6 were waited for; matrix products, arithmetic and copies ran while one was open for 0% of the time, Pallas kernels for 0%

profile of v1, /device:TPU:16, one launch (start us, length us, event | category | flops | bytes accessed | tf_op | source)
XLA Modules:
  0.0 246.9 jit_solution(813136822619654408)
XLA Ops:
  0.0 0.0 copy-start
  0.0 4.2 %copy.11 = bf16[128,8192]{0,1:T(8,128)(2,1)} copy(bf16[128,8192]{1,0:T(8,128)(2,1)} %param.5) | data formatting | bytes 4194304 | tf_op jit(solution)/shard_map/reshape | solution.py:28
  4.2 4.1 %copy.12 = bf16[128,8192]{0,1:T(8,128)(2,1)} copy(bf16[128,8192]{1,0:T(8,128)(2,1)} %param.6) | data formatting | bytes 4194304 | tf_op jit(solution)/shard_map/reshape | solution.py:29
  8.3 3.8 %convolution_convert_fusion = bf16[64,128,128]{2,1,0:T(8,128)(2,1)S(1)} fusion(bf16[128,64,128]{0,2,1:T(8,128)(2,1)} %bitcast.108, bf16[128,64,128]{0,2,1:T(8,128)(2,1)} %bitcast.110), kind=kOutput, calls=%fused_computation.7 | convolution fusion | flops 269484032 | bytes 6291456 | tf_op jit(solution)/shard_map/bhd,bhe->hde/dot_general | solution.py:30
  12.1 59.5 %all_to_all.10 = bf16[8,8,128,128]{3,2,1,0:T(8,128)(2,1)S(1)} all-to-all(bf16[8,8,128,128]{3,2,1,0:T(8,128)(2,1)S(1)} %bitcast.113), channel_id=1, replica_groups=mesh['seq'=32,'head'=8] {'head'}, dimensions={0} | all-to-all | bytes 4194304 | tf_op jit(solution)/shard_map/all_to_all | solution.py:31
  71.5 0.4 convert_reduce_fusion
  71.9 1.9 collective-permute-start
  73.8 10.7 %collective-permute-done = f32[8,128,128]{2,1,0:T(8,128)S(1)} collective-permute-done((f32[8,128,128]{2,1,0:T(8,128)S(1)}, f32[8,128,128]{2,1,0:T(8,128)S(1)}, u32[]{:S(2)}, u32[]{:S(2)}) %collective-permute-start) | collective-permute-done | bytes 524320 | tf_op jit(solution)/shard_map/ppermute | solution.py:12
  84.5 0.1 add.50
  84.6 1.9 collective-permute-start.1
  86.5 12.9 %collective-permute-done.1 = f32[8,128,128]{2,1,0:T(8,128)S(1)} collective-permute-done((f32[8,128,128]{2,1,0:T(8,128)S(1)}, f32[8,128,128]{2,1,0:T(8,128)S(1)}, u32[]{:S(2)}, u32[]{:S(2)}) %collective-permute-start.1) | collective-permute-done | bytes 524320 | tf_op jit(solution)/shard_map/ppermute | solution.py:12
  99.4 0.1 add.51
  99.5 2.5 %collective-permute-start.2 = (f32[8,128,128]{2,1,0:T(8,128)S(1)}, f32[8,128,128]{2,1,0:T(8,128)S(1)}, u32[]{:S(2)}, u32[]{:S(2)}) collective-permute-start(f32[8,128,128]{2,1,0:T(8,128)S(1)} %add.51), channel_id=1, source_target_pairs={{0,32},{8,40},{16,48},{24,56},{32,64},{40,72},{48,80},{56,88},{64,... | collective-permute-start | bytes 1572872 | tf_op jit(solution)/shard_map/ppermute | solution.py:12
  102.0 11.8 %collective-permute-done.2 = f32[8,128,128]{2,1,0:T(8,128)S(1)} collective-permute-done((f32[8,128,128]{2,1,0:T(8,128)S(1)}, f32[8,128,128]{2,1,0:T(8,128)S(1)}, u32[]{:S(2)}, u32[]{:S(2)}) %collective-permute-start.2) | collective-permute-done | bytes 524320 | tf_op jit(solution)/shard_map/ppermute | solution.py:12
  113.8 0.1 add.52
  113.8 3.2 %collective-permute-start.3 = (f32[8,128,128]{2,1,0:T(8,128)S(1)}, f32[8,128,128]{2,1,0:T(8,128)S(1)}, u32[]{:S(2)}, u32[]{:S(2)}) collective-permute-start(f32[8,128,128]{2,1,0:T(8,128)S(1)} %add.52), channel_id=1, source_target_pairs={{0,64},{8,72},{16,80},{24,88},{32,96},{40,104},{48,112},{56,120},{... | collective-permute-start | bytes 1572872 | tf_op jit(solution)/shard_map/ppermute | solution.py:12
  117.0 8.0 %collective-permute-done.3 = f32[8,128,128]{2,1,0:T(8,128)S(1)} collective-permute-done((f32[8,128,128]{2,1,0:T(8,128)S(1)}, f32[8,128,128]{2,1,0:T(8,128)S(1)}, u32[]{:S(2)}, u32[]{:S(2)}) %collective-permute-start.3) | collective-permute-done | bytes 524320 | tf_op jit(solution)/shard_map/ppermute | solution.py:12
  125.0 0.1 add.53
  125.1 1.3 collective-permute-start.4
  126.4 11.3 %collective-permute-done.4 = f32[8,128,128]{2,1,0:T(8,128)S(1)} collective-permute-done((f32[8,128,128]{2,1,0:T(8,128)S(1)}, f32[8,128,128]{2,1,0:T(8,128)S(1)}, u32[]{:S(2)}, u32[]{:S(2)}) %collective-permute-start.4) | collective-permute-done | bytes 524320 | tf_op jit(solution)/shard_map/ppermute | solution.py:12
  137.6 0.1 add.54
  137.7 1.9 collective-permute-start.5
  139.6 0.5 convert_element_type.37
  140.1 10.2 %collective-permute-done.5 = f32[8,128,128]{2,1,0:T(8,128)S(1)} collective-permute-done((f32[8,128,128]{2,1,0:T(8,128)S(1)}, f32[8,128,128]{2,1,0:T(8,128)S(1)}, u32[]{:S(2)}, u32[]{:S(2)}) %collective-permute-start.5) | collective-permute-done | bytes 524320 | tf_op jit(solution)/shard_map/ppermute | solution.py:12
  150.3 0.7 bitcast_dynamic-update-slice_fusion.6
  151.0 0.8 bitcast_dynamic-update-slice_fusion.5
  151.8 0.8 bitcast_dynamic-update-slice_fusion.4
  152.6 0.8 bitcast_dynamic-update-slice_fusion.3
  153.4 0.8 bitcast_dynamic-update-slice_fusion.2
  154.2 0.8 bitcast_dynamic-update-slice_fusion.1
  154.9 0.8 bitcast_dynamic-update-slice_fusion
  155.7 0.8 fusion.16
  156.5 0.0 copy-start.1
  156.5 4.5 %all-to-all-start.1 = ((bf16[8,8,128,128]{3,2,1,0:T(8,128)(2,1)}), bf16[8,8,128,128]{3,2,1,0:T(8,128)(2,1)}, u32[]{:S(2)}, u32[]{:S(2)}) async-start(bf16[8,8,128,128]{3,2,1,0:T(8,128)(2,1)} %fusion.16), calls=%async_computation.1 | async-start | bytes 4194304 | tf_op jit(solution)/shard_map/all_to_all | solution.py:41
  161.0 0.0 copy-done.1
  161.0 65.2 %all_gather.3 = f32[64,128]{1,0:T(8,128)S(1)} all-gather(f32[8,128]{1,0:T(8,128)S(1)} %copy-done.1), channel_id=1, replica_groups=mesh['seq'=32,'head'=8] {'head'}, dimensions={0}, use_global_device_ids=true | all-gather | bytes 36864 | tf_op jit(solution)/shard_map/all_gather | solution.py:34
  226.2 0.0 all-to-all-done.1
  226.2 0.0 copy-done
  226.3 5.1 %fusion.1 = f32[64,128,128]{2,1,0:T(8,128)} fusion(bf16[64,128,128]{2,1,0:T(8,128)(2,1)} %bitcast.21, bf16[128,8192]{1,0:T(8,128)(2,1)S(1)} %copy-done), kind=kOutput, calls=%fused_computation.5 | convolution fusion | flops 268435456 | bytes 8388608 | tf_op jit(solution)/shard_map/bhd,hde->bhe/dot_general | solution.py:43
  231.4 7.6 %multiply_reduce_fusion = (f32[128,64]{0,1:T(8,128)S(1)}, f32[128,64,128]{0,2,1:T(8,128)}) fusion(bf16[128,64,128]{0,2,1:T(8,128)(2,1)} %bitcast.111, bf16[128,64,128]{0,2,1:T(8,128)(2,1)} %bitcast.109, pred[128,128]{1,0:T(8,128)(4,1)S(1)} %iota_compare_fusion, f32[64,128,128]{2,1,0:T(8,128)} %fusion.1, bf16[128,8192]{1,0:T(8,128)(2,1)S(1)} %copy-done), kind=kOutput, calls=%fused_computation.2 | convolution fusion | flops 542105600 | bytes 14729216 | tf_op jit(solution)/shard_map/hbc,chd->bhd/dot_general | solution.py:47
  239.0 3.9 %multiply_convert_fusion = bf16[128,64,128]{0,2,1:T(8,128)(2,1)} fusion(f32[128,64,128]{0,2,1:T(8,128)} %get-tuple-element.10, f32[64,128]{1,0:T(8,128)S(1)} %all_gather.3, f32[128,64]{0,1:T(8,128)S(1)} %add_rsqrt_fusion), kind=kLoop, calls=%fused_computation.1 | loop fusion | flops 3145728 | bytes 6356992 | tf_op jit(solution)/shard_map/convert_element_type | solution.py:50
  242.9 4.1 %copy.10 = bf16[128,8192]{1,0:T(8,128)(2,1)} copy(bf16[128,8192]{0,1:T(8,128)(2,1)} %bitcast.112) | data formatting | bytes 4194304 | tf_op jit(solution)/shard_map/reshape | solution.py:51
  (2 shorter events, 0.0 us)
Async XLA Ops:
  0.0 226.2 %copy-start = (bf16[128,8192]{1,0:T(8,128)(2,1)S(1)}, bf16[128,8192]{1,0:T(8,128)(2,1)}, u32[]{:S(2)}) copy-start(bf16[128,8192]{1,0:T(8,128)(2,1)} %param.4) | copy-start | bytes 6291460
  71.9 12.6 %collective-permute-start = (f32[8,128,128]{2,1,0:T(8,128)S(1)}, f32[8,128,128]{2,1,0:T(8,128)S(1)}, u32[]{:S(2)}, u32[]{:S(2)}) collective-permute-start(f32[8,128,128]{2,1,0:T(8,128)S(1)} %convert_reduce_fusion), channel_id=1, source_target_pairs={{0,8},{8,16},{16,24},{24,32},{32,40},{40,48},{48,56},{56,64},{64,7... | collective-permute-start | bytes 1572872 | tf_op jit(solution)/shard_map/ppermute | solution.py:12
  84.6 14.8 %collective-permute-start.1 = (f32[8,128,128]{2,1,0:T(8,128)S(1)}, f32[8,128,128]{2,1,0:T(8,128)S(1)}, u32[]{:S(2)}, u32[]{:S(2)}) collective-permute-start(f32[8,128,128]{2,1,0:T(8,128)S(1)} %add.50), channel_id=1, source_target_pairs={{0,16},{8,24},{16,32},{24,40},{32,48},{40,56},{48,64},{56,72},{64,... | collective-permute-start | bytes 1572872 | tf_op jit(solution)/shard_map/ppermute | solution.py:12
  99.5 14.3 %collective-permute-start.2 = (f32[8,128,128]{2,1,0:T(8,128)S(1)}, f32[8,128,128]{2,1,0:T(8,128)S(1)}, u32[]{:S(2)}, u32[]{:S(2)}) collective-permute-start(f32[8,128,128]{2,1,0:T(8,128)S(1)} %add.51), channel_id=1, source_target_pairs={{0,32},{8,40},{16,48},{24,56},{32,64},{40,72},{48,80},{56,88},{64,... | collective-permute-start | bytes 1572872 | tf_op jit(solution)/shard_map/ppermute | solution.py:12
  113.8 11.2 %collective-permute-start.3 = (f32[8,128,128]{2,1,0:T(8,128)S(1)}, f32[8,128,128]{2,1,0:T(8,128)S(1)}, u32[]{:S(2)}, u32[]{:S(2)}) collective-permute-start(f32[8,128,128]{2,1,0:T(8,128)S(1)} %add.52), channel_id=1, source_target_pairs={{0,64},{8,72},{16,80},{24,88},{32,96},{40,104},{48,112},{56,120},{... | collective-permute-start | bytes 1572872 | tf_op jit(solution)/shard_map/ppermute | solution.py:12
  125.1 12.6 %collective-permute-start.4 = (f32[8,128,128]{2,1,0:T(8,128)S(1)}, f32[8,128,128]{2,1,0:T(8,128)S(1)}, u32[]{:S(2)}, u32[]{:S(2)}) collective-permute-start(f32[8,128,128]{2,1,0:T(8,128)S(1)} %add.53), channel_id=1, source_target_pairs={{0,128},{8,136},{16,144},{24,152},{32,160},{40,168},{48,176},{56,1... | collective-permute-start | bytes 1572872 | tf_op jit(solution)/shard_map/ppermute | solution.py:12
  137.7 12.6 %collective-permute-start.5 = (f32[8,128,128]{2,1,0:T(8,128)S(1)}, f32[8,128,128]{2,1,0:T(8,128)S(1)}, u32[]{:S(2)}, u32[]{:S(2)}) collective-permute-start(f32[8,128,128]{2,1,0:T(8,128)S(1)} %add.54), channel_id=1, source_target_pairs={{0,8},{8,16},{16,24},{24,32},{32,40},{40,48},{48,56},{56,64},{64,7... | collective-permute-start | bytes 1572872 | tf_op jit(solution)/shard_map/ppermute | solution.py:12
  156.5 4.5 %copy-start.1 = (f32[8,128]{1,0:T(8,128)S(1)}, f32[8,128]{1,0:T(8,128)}, u32[]{:S(2)}) copy-start(f32[8,128]{1,0:T(8,128)} %param.7) | copy-start | bytes 12292
  156.5 69.7 %all-to-all-start.1 = ((bf16[8,8,128,128]{3,2,1,0:T(8,128)(2,1)}), bf16[8,8,128,128]{3,2,1,0:T(8,128)(2,1)}, u32[]{:S(2)}, u32[]{:S(2)}) async-start(bf16[8,8,128,128]{3,2,1,0:T(8,128)(2,1)} %fusion.16), calls=%async_computation.1 | async-start | bytes 4194304 | tf_op jit(solution)/shard_map/all_to_all | solution.py:41

commit v2 on v1

v2 whole, which is shorter than its diff:
```python
import functools

import jax
import jax.numpy as jnp
from jax import lax
from jax.experimental import pallas as pl
from jax.experimental.pallas import tpu as pltpu
from jax.sharding import PartitionSpec as P

HEADS = 64
HD = 128
TOK = 128
Z = 8
LINE = 16
CHUNKS = HEADS // LINE
MESH = pl.DeviceIdType.MESH
BF16 = jnp.bfloat16
F32 = jnp.float32


def columns(head):
    return pl.ds(pl.multiple_of(head * HD, HD), HD)


def kernel(
    q_ref,
    k_ref,
    v_ref,
    gain_ref,
    out_ref,
    state_send,
    state_recv,
    row_send,
    row_recv,
    col_send,
    col_recv,
    carry_send,
    carry_recv,
    gain_all,
    intra,
    state_ssem,
    state_rsem,
    row_ssem,
    row_rsem,
    col_ssem,
    col_rsem,
    carry_ssem,
    carry_rsem,
    gain_ssem,
    gain_rsem,
):
    seq = lax.axis_index("seq")
    z = lax.axis_index("head")
    core = lax.rem(seq, 2)
    chip = seq - core
    x = lax.rem(seq // 2, 4)
    y = seq // 8
    me = core * Z + z

    def line_peer(dz, dc):
        other_core = lax.rem(core + dc, 2)
        other_z = lax.rem(z + dz, Z)
        return (chip + other_core, other_z), other_core * Z + other_z

    def row_peer(d):
        other = lax.rem(x + d, 4)
        return (y * 8 + other * 2 + core, z), other

    def col_peer(d):
        other = lax.rem(y + d, 4)
        return (other * 8 + x * 2 + core, z), other

    offsets = [(dz, dc) for dz in (4, 3, 5, 2, 6, 1, 7, 0) for dc in (0, 1) if (dz, dc) != (0, 0)]

    barrier = pltpu.get_barrier_semaphore()
    for dz, dc in offsets:
        pl.semaphore_signal(barrier, inc=1, device_id=line_peer(dz, dc)[0], device_id_type=MESH)
    for d in (1, 2, 3):
        pl.semaphore_signal(barrier, inc=1, device_id=row_peer(d)[0], device_id_type=MESH)
        pl.semaphore_signal(barrier, inc=1, device_id=col_peer(d)[0], device_id_type=MESH)
    pl.semaphore_wait(barrier, len(offsets) + 6)

    def gain_copy(dz):
        target, _ = line_peer(dz, 0)
        return pltpu.make_async_remote_copy(
            src_ref=gain_ref,
            dst_ref=gain_all.at[z],
            send_sem=gain_ssem.at[target[1]],
            recv_sem=gain_rsem.at[z],
            device_id=target,
            device_id_type=MESH,
        )

    def gain_arrival(dz):
        source = lax.rem(z + dz, Z)
        return pltpu.make_async_remote_copy(
            src_ref=gain_ref,
            dst_ref=gain_all.at[source],
            send_sem=gain_ssem.at[source],
            recv_sem=gain_rsem.at[source],
            device_id=line_peer(dz, 0)[0],
            device_id_type=MESH,
        )

    def line_copy(send, recv, ssem, rsem, j, dz, dc, slot):
        target, index = line_peer(dz, dc)
        return pltpu.make_async_remote_copy(
            src_ref=send.at[j, index],
            dst_ref=recv.at[j, slot(index)],
            send_sem=ssem.at[j, index],
            recv_sem=rsem.at[j, slot(index)],
            device_id=target,
            device_id_type=MESH,
        )

    mine = lambda index: me
    theirs = lambda index: index

    def side_copy(send, recv, ssem, rsem, j, peer, slot, d):
        return pltpu.make_async_remote_copy(
            src_ref=send.at[j],
            dst_ref=recv.at[j, slot],
            send_sem=ssem.at[j, d],
            recv_sem=rsem.at[j, slot],
            device_id=peer,
            device_id_type=MESH,
        )

    def make_states(j):
        def state(index):
            cols = columns(index * CHUNKS + j)
            return lax.dot_general(
                k_ref[:, cols], v_ref[:, cols], (((0,), (0,)), ((), ())), preferred_element_type=F32
            ).astype(BF16)

        for dz, dc in offsets:
            _, index = line_peer(dz, dc)
            state_send[j, index] = state(index)
            line_copy(state_send, state_recv, state_ssem, state_rsem, j, dz, dc, mine).start()
        state_recv[j, me] = state(me)

    def reduce_line(j):
        for dz, dc in offsets:
            line_copy(state_send, state_recv, state_ssem, state_rsem, j, dz, dc, theirs).wait_recv()
        total = state_recv[j, 0].astype(F32)
        for index in range(1, LINE):
            total = total + state_recv[j, index].astype(F32)
        row_send[j] = total
        for d in (1, 2, 3):
            side_copy(row_send, row_recv, row_ssem, row_rsem, j, row_peer(d)[0], x, d).start()

    def reduce_row(j):
        for d in (1, 2, 3):
            peer, other = row_peer(d)
            side_copy(row_send, row_recv, row_ssem, row_rsem, j, peer, other, d).wait_recv()
        total = row_send[j]
        before = jnp.zeros((HD, HD), F32)
        for d in (1, 2, 3):
            _, other = row_peer(d)
            value = row_recv[j, other]
            total = total + value
            before = before + jnp.where(other < x, value, 0.0)
        col_send[j] = total
        row_recv[j, x] = before
        for d in (1, 2, 3):
            side_copy(col_send, col_recv, col_ssem, col_rsem, j, col_peer(d)[0], y, d).start()

    def spread(j):
        for d in (1, 2, 3):
            peer, other = col_peer(d)
            side_copy(col_send, col_recv, col_ssem, col_rsem, j, peer, other, d).wait_recv()
        running = row_recv[j, x]
        for d in (1, 2, 3):
            _, other = col_peer(d)
            running = running + jnp.where(other < y, col_recv[j, other], 0.0)
        for index in range(LINE):
            carry_send[j, index] = running.astype(BF16)
            running = running + state_recv[j, index].astype(F32)
        for dz, dc in offsets:
            line_copy(carry_send, carry_recv, carry_ssem, carry_rsem, j, dz, dc, mine).start()
        carry_recv[j, me] = carry_send[j, me]

    causal = lax.broadcasted_iota(jnp.int32, (TOK, TOK), 0) >= lax.broadcasted_iota(jnp.int32, (TOK, TOK), 1)

    def local_heads(j):
        for index in range(LINE):
            cols = columns(index * CHUNKS + j)
            scores = lax.dot_general(
                q_ref[:, cols], k_ref[:, cols], (((1,), (1,)), ((), ())), preferred_element_type=F32
            )
            scores = jnp.where(causal, scores, 0.0).astype(BF16)
            intra[:, cols] = jnp.dot(scores, v_ref[:, cols], preferred_element_type=F32)

    def finish(j):
        for dz, dc in offsets:
            line_copy(carry_send, carry_recv, carry_ssem, carry_rsem, j, dz, dc, theirs).wait_recv()
        for index in range(LINE):
            owner = index
            head = (index * CHUNKS) + j
            cols = columns(head)
            raw = intra[:, cols] + jnp.dot(q_ref[:, cols], carry_recv[j, owner], preferred_element_type=F32)
            scale = lax.rsqrt(jnp.mean(raw * raw, axis=-1, keepdims=True) + 1e-06)
            gain = gain_all[index * CHUNKS // 8, pl.ds(lax.rem(index * CHUNKS, 8) + j, 1), :]
            out_ref[:, cols] = (raw * scale * gain).astype(BF16)

    for dz in range(1, Z):
        gain_copy(dz).start()
    gain_all[z] = gain_ref[...]

    lax.fori_loop(0, CHUNKS, lambda j, _: (make_states(j), None)[1], None)
    lax.fori_loop(0, CHUNKS, lambda j, _: (local_heads(j), None)[1], None)

    def wave(t, _):
        @pl.when(t < CHUNKS)
        def _():
            reduce_line(t)

        @pl.when(jnp.logical_and(t >= 2, t < CHUNKS + 2))
        def _():
            spread(t - 2)

        @pl.when(jnp.logical_and(t >= 1, t < CHUNKS + 1))
        def _():
            reduce_row(t - 1)

    lax.fori_loop(0, CHUNKS + 2, wave, None)
    for dz in range(1, Z):
        gain_arrival(dz).wait_recv()
    lax.fori_loop(0, CHUNKS, lambda j, _: (finish(j), None)[1], None)

    def drain(j, _):
        for dz, dc in offsets:
            line_copy(state_send, state_recv, state_ssem, state_rsem, j, dz, dc, mine).wait_send()
            line_copy(carry_send, carry_recv, carry_ssem, carry_rsem, j, dz, dc, mine).wait_send()
        for d in (1, 2, 3):
            side_copy(row_send, row_recv, row_ssem, row_rsem, j, row_peer(d)[0], x, d).wait_send()
            side_copy(col_send, col_recv, col_ssem, col_rsem, j, col_peer(d)[0], y, d).wait_send()

    lax.fori_loop(0, CHUNKS, drain, None)
    for dz in range(1, Z):
        gain_copy(dz).wait_send()


def per_device(queries, key_vectors, value_vectors, out_gain):
    vmem = pl.BlockSpec(memory_space=pltpu.VMEM)
    dma = pltpu.SemaphoreType.DMA
    return pl.pallas_call(
        kernel,
        out_shape=jax.ShapeDtypeStruct((TOK, HEADS * HD), BF16),
        in_specs=[vmem] * 4,
        out_specs=vmem,
        scratch_shapes=[
            pltpu.VMEM((CHUNKS, LINE, HD, HD), BF16),
            pltpu.VMEM((CHUNKS, LINE, HD, HD), BF16),
            pltpu.VMEM((CHUNKS, HD, HD), F32),
            pltpu.VMEM((CHUNKS, 4, HD, HD), F32),
            pltpu.VMEM((CHUNKS, HD, HD), F32),
            pltpu.VMEM((CHUNKS, 4, HD, HD), F32),
            pltpu.VMEM((CHUNKS, LINE, HD, HD), BF16),
            pltpu.VMEM((CHUNKS, LINE, HD, HD), BF16),
            pltpu.VMEM((Z, 8, HD), F32),
            pltpu.VMEM((TOK, HEADS * HD), F32),
            dma((CHUNKS, LINE)),
            dma((CHUNKS, LINE)),
            dma((CHUNKS, 4)),
            dma((CHUNKS, 4)),
            dma((CHUNKS, 4)),
            dma((CHUNKS, 4)),
            dma((CHUNKS, LINE)),
            dma((CHUNKS, LINE)),
            dma((Z,)),
            dma((Z,)),
        ],
        compiler_params=pltpu.CompilerParams(
            collective_id=0, has_side_effects=True, vmem_limit_bytes=48 * 1024 * 1024
        ),
    )(queries, key_vectors, value_vectors, out_gain)


def solution(mesh):
    return jax.shard_map(
        per_device,
        mesh=mesh,
        in_specs=(
            P(("seq", "head"), None),
            P(("seq", "head"), None),
            P(("seq", "head"), None),
            P("head", None),
        ),
        out_specs=P(("seq", "head"), None),
        check_vma=False,
    )
```

time: 248 us -> 111 us (0.45)
  blocking collectives: 125 us -> 0 us
  Pallas kernels: 0 us -> 106 us
  waiting for transfers between devices: 64.8 us -> 0 us
  starting transfers between devices: 17.2 us -> 0 us
  matrix products: 16.5 us -> 0 us
  other arithmetic: 11.3 us -> 0 us
  local copies, waits for them, and re-layouts: 12.3 us -> 3.6 us
    pallas_call x0 -> x1, Pallas kernels: none -> 106 us  [per_device(): pl.pallas_call(kernel, out_shape=jax.ShapeDtypeStruct((TOK, HEADS * HD),...]
    all_gather x1 -> x0, blocking collectives: 65.2 us -> none  [per_device(): gain = lax.all_gather(out_gain, 'head', axis=0, tiled=True)]
    ppermute x6 -> x0, waiting for transfers between devices: 64.8 us -> none  [shifted(): lax.ppermute(block, axis, [(i, i + distance) for i in range(count - dista...]
    all_to_all x1 -> x0, blocking collectives: 59.5 us -> none  [per_device(): lax.all_to_all(states.astype(jnp.bfloat16).reshape(8, HEADS // 8, HD, HD)...]
    dot_general x3 -> x0, matrix products: 16.5 us -> none  [the longest x1 7.56 us: per_device(): jnp.einsum('hbc,chd->bhd', scores, value_heads, preferred_element_type=jn...]
    ppermute x6 -> x0, starting transfers between devices: 12.8 us -> none  [shifted(): lax.ppermute(block, axis, [(i, i + distance) for i in range(count - dista...]
    reshape x3 -> x0, local copies, waits for them, and re-layouts: 12.3 us -> none  [the longest x1 4.21 us: per_device(): key_heads = key_vectors.reshape(tokens, HEADS, HD)]
    unnamed x7 -> x0, other arithmetic: 5.4 us -> none
  transfers between devices with their start and end apart: 7 -> 0, of which waited for: 6 -> 0; matrix products, arithmetic and copies ran while one was open for 0% -> 0% of each run, Pallas kernels for 0% -> 0%
where the time goes in v2:
time: 111 us; the launch traced here: 110 us
  Pallas kernels  106 us (95%)
  local copies, waits for them, and re-layouts  3.6 us (3%)
    pallas_call x1, Pallas kernels, per_device(): pl.pallas_call(kernel, out_shape=jax.ShapeDtypeStruct((TOK, HEADS * HD),...  106 us
    unnamed x5, local copies, waits for them, and re-layouts  3.6 us

profile of v2, /device:TPU:16, one launch (start us, length us, event | category | flops | bytes accessed | tf_op | source)
XLA Modules:
  0.0 109.8 jit_solution(16345569453791867883)
XLA Ops:
  0.0 0.0 copy-start
  0.0 1.6 %copy-done = bf16[128,8192]{1,0:T(8,128)(2,1)S(1)} copy-done((bf16[128,8192]{1,0:T(8,128)(2,1)S(1)}, bf16[128,8192]{1,0:T(8,128)(2,1)}, u32[]{:S(2)}) %copy-start) | copy-done | bytes 2097176
  1.6 0.0 copy-start.1
  1.6 0.7 copy-done.1
  2.3 106.2 %shard_map.46 = bf16[128,8192]{1,0:T(8,128)(2,1)S(1)} custom-call(bf16[128,8192]{1,0:T(8,128)(2,1)S(1)} %copy-done, bf16[128,8192]{1,0:T(8,128)(2,1)} %k_ref.1, bf16[128,8192]{1,0:T(8,128)(2,1)} %v_ref.1, f32[8,128]{1,0:T(8,128)S(1)} %copy-done.1), custom_call_target="tpu_custom_call" | custom-call | tf_op jit(solution)/shard_map/pallas_call | solution.py:247
  108.5 1.3 %copy.6 = bf16[128,8192]{1,0:T(8,128)(2,1)} copy(bf16[128,8192]{1,0:T(8,128)(2,1)S(1)} %shard_map.46) | data formatting | bytes 4194304
Async XLA Ops:
  0.0 1.6 %copy-start = (bf16[128,8192]{1,0:T(8,128)(2,1)S(1)}, bf16[128,8192]{1,0:T(8,128)(2,1)}, u32[]{:S(2)}) copy-start(bf16[128,8192]{1,0:T(8,128)(2,1)} %q_ref.1) | copy-start | bytes 6291460
  1.6 0.7 copy-start.1
